TPU v7x, 128 devices: a whole 4x4x4 slice. The times are simulated.
128 devices in a mesh: frame: 8 (over y, core), strip: 16 (over x, z).
Axes of the slice: x: 4, y: 4, z: 4, core: 2. Of those that a mesh axis runs over, the one named last changes fastest.
Arguments:
- tokens: bfloat16 [8, 32, 128, 768], P('frame', 'strip'), may hold values from -6 to 6
- timestep: int32 [1], replicated, may hold values from 0 to 999
- col_order: int32 [128], replicated, may hold values from 0 to 127, each once
- row_order: int32 [32], replicated, may hold values from 0 to 31, each once
- w_time: bfloat16 [256, 3072], replicated, may hold values from -0.375 to 0.375
- w_in: bfloat16 [2, 768, 3328], replicated, may hold values from -0.21875 to 0.21875
- w_dt: bfloat16 [2, 768, 24], replicated, may hold values from -0.21875 to 0.21875
- conv_w: float32 [2, 4, 1792], replicated, may hold values from -0.5 to 0.5
- conv_b: float32 [2, 1792], replicated, may hold values from -3 to 3
- dt_bias: float32 [2, 24], replicated, may hold values from -1 to 0.5
- a_log: float32 [2, 24], replicated
- d_skip: float32 [2, 24], replicated, may hold values from 0.5 to 2
- out_gain: float32 [2, 1536], replicated, may hold values from 0.1 to 1.9
- w_out: bfloat16 [2, 1536, 768], replicated, may hold values from -0.15625 to 0.15625
Outputs:
- denoised: bfloat16 [8, 32, 128, 768], P('frame', None, 'strip')
Inputs may be any that keep to these rules, and one draw needn't show every extreme that they name: `col_order`: a permutation. `row_order`: a permutation.
All inputs are finite; a program needn't handle non-finite values.
Results may differ from a plain program's by a relative error of at most 0.015.
Values may be sent and summed in bfloat16 or wider, within the bound.
A program may use at most 256 MiB of HBM per device.

v0:
```python
import math

import jax
import jax.numpy as jnp
from jax import lax
from jax.sharding import PartitionSpec as P

HEADS = 24
HDIM = 64
STATE = 128
CONV = 4
GROUP = 256
INNER = 1536


EPS_TOKEN = 1e-06
EPS_HEAD = 1e-05


def shifted(value, axis, steps):
    count = lax.axis_size(axis)
    first, last = (max(0, -steps), min(count, count - steps))
    return lax.ppermute(value, axis, [(source, source + steps) for source in range(first, last)])


def prefix(value, axis, join, neutral):
    count, mine = (lax.axis_size(axis), lax.axis_index(axis))
    pieces = jax.tree.map(lambda part: lax.all_gather(part, axis), value)
    subtotal = jax.tree.map(
        lambda part, zero: jnp.full_like(part, 0) + jnp.asarray(zero, part.dtype), value, neutral
    )

    def turn(position, subtotal):
        longer = join(subtotal, jax.tree.map(lambda part: part[position], pieces))
        return jax.tree.map(lambda new, old: jnp.where(position < mine, new, old), longer, subtotal)

    return lax.fori_loop(0, count - 1, turn, subtotal)


def time_condition(timestep, w_time):
    half_freq = w_time.shape[0] // 2
    ladder = jnp.arange(half_freq).astype(jnp.float32)
    frequency = jnp.exp(-math.log(10000.0) * ladder / half_freq)
    angles = timestep.astype(jnp.float32)[:, None] * frequency[None, :]
    feature = jnp.concatenate([jnp.cos(angles), jnp.sin(angles)], axis=1)
    feature = jax.nn.silu(feature).astype(jnp.bfloat16)
    return jnp.dot(feature, w_time, preferred_element_type=jnp.float32)[0]


def modulate(sequence, condition, layer_index):
    model_width = sequence.shape[-1]
    values = sequence.astype(jnp.float32)
    scaled = values * lax.rsqrt(jnp.mean(values * values, axis=-1, keepdims=True) + EPS_TOKEN)
    factor = condition[2 * layer_index * model_width : (2 * layer_index + 1) * model_width]
    offset = condition[(2 * layer_index + 1) * model_width : (2 * layer_index + 2) * model_width]
    return (scaled * (1.0 + factor) + offset).astype(jnp.bfloat16)


def project(normed, w_in, w_dt, dt_bias, layer_index):
    projected = jnp.dot(normed, w_in[layer_index], preferred_element_type=jnp.float32)
    raw_step = jnp.dot(normed, w_dt[layer_index], preferred_element_type=jnp.float32)
    return (projected, jax.nn.softplus(raw_step + dt_bias[layer_index]))


def odd_lines(line_count, first_index, rank):
    parity = (first_index + jnp.arange(line_count)) % 2 == 1
    return parity.reshape((line_count,) + (1,) * (rank - 1))


def into_order(block, order, first_index):
    gathered = jnp.take(block, order, axis=1)
    odd_mask = odd_lines(block.shape[0], first_index, block.ndim)
    return jnp.where(odd_mask, jnp.flip(gathered, axis=1), gathered)


def from_order(block, order, first_index):
    odd_mask = odd_lines(block.shape[0], first_index, block.ndim)
    unflipped = jnp.where(odd_mask, jnp.flip(block, axis=1), block)
    places = jnp.zeros_like(order).at[order].set(jnp.arange(order.shape[0]))
    return jnp.take(unflipped, places, axis=1)


def block_terms(x_heads, b_rows, c_rows, step_size, rates):
    cumulative = jnp.cumsum(step_size * rates, axis=1)
    cum_heads = jnp.swapaxes(cumulative, 1, 2)
    step_heads = jnp.swapaxes(step_size, 1, 2)
    scores = jnp.einsum("ntk,nsk->nts", c_rows, b_rows, preferred_element_type=jnp.float32)
    length = step_size.shape[1]
    lower_mask = jnp.arange(length)[:, None] >= jnp.arange(length)[None, :]
    log_gap = cum_heads[:, :, :, None] - cum_heads[:, :, None, :]
    decay_factor = jnp.exp(jnp.where(lower_mask, log_gap, -jnp.inf))
    mixing = (scores[:, None] * decay_factor * step_heads[:, :, None, :]).astype(jnp.bfloat16)
    inside = jnp.einsum("nhts,nshp->nthp", mixing, x_heads, preferred_element_type=jnp.float32)
    to_end = jnp.exp(cum_heads[:, :, -1:] - cum_heads) * step_heads
    weighted = (x_heads.astype(jnp.float32) * jnp.swapaxes(to_end, 1, 2)[..., None]).astype(
        jnp.bfloat16
    )
    block_state = jnp.einsum("nshp,nsk->nhpk", weighted, b_rows, preferred_element_type=jnp.float32)
    return (inside, block_state, cumulative, cum_heads[:, :, -1])


def combine(earlier, later):
    return (earlier[0] + later[0], earlier[1] * jnp.exp(later[0])[:, None, None] + later[1])


def mixer(seq_x, projected, step_size, params, layer_index):
    w_in, w_dt, conv_w, conv_b, dt_bias, a_log, d_skip, out_gain, w_out = params
    length = seq_x.shape[0]
    blocks = length // GROUP
    gate_z = projected[:, :INNER]
    conv_in = projected[:, INNER:]
    conv_tail = shifted(conv_in[length - (CONV - 1) :], ("frame", "strip"), 1)
    padded = jnp.concatenate([conv_tail, conv_in], axis=0)
    conved = conv_b[layer_index]
    for tap_index in range(CONV):
        conved = conved + conv_w[layer_index, tap_index] * padded[tap_index : tap_index + length]
    conved = jax.nn.silu(conved).astype(jnp.bfloat16)
    x_heads = conved[:, :INNER].reshape(blocks, GROUP, HEADS, HDIM)
    b_rows = conved[:, INNER : INNER + STATE].reshape(blocks, GROUP, STATE)
    c_rows = conved[:, INNER + STATE :].reshape(blocks, GROUP, STATE)
    rates = -jnp.exp(a_log[layer_index])
    inside, block_state, cumulative, decay_total = block_terms(
        x_heads, b_rows, c_rows, step_size.reshape(blocks, GROUP, HEADS), rates
    )

    def advance(carried_in, pieces):
        entering, decayed = carried_in
        state_piece, block_decay = pieces
        return (
            (jnp.exp(block_decay)[:, None, None] * entering + state_piece, decayed + block_decay),
            (entering, decayed),
        )

    zero_state = jnp.zeros((HEADS, HDIM, STATE), jnp.float32)
    zero_decay = jnp.zeros((HEADS,), jnp.float32)
    summary, prefixes = lax.scan(advance, (zero_state, zero_decay), (block_state, decay_total))
    local_end, device_decay = summary
    local_enter, prefix_decay = prefixes
    identity = (zero_decay, zero_state)
    own_summary = (device_decay, local_end)
    incoming = prefix(own_summary, ("frame", "strip"), combine, identity)
    enter_total = local_enter + jnp.exp(prefix_decay)[:, :, None, None] * incoming[1][None]
    carried_part = jnp.exp(cumulative)[..., None] * jnp.einsum(
        "nck,nhpk->nchp", c_rows.astype(jnp.float32), enter_total, precision=lax.Precision.HIGHEST
    )
    ssd_out = (
        inside
        + carried_part
        + d_skip[layer_index][None, None, :, None] * x_heads.astype(jnp.float32)
    )
    gated = ssd_out.reshape(length, HEADS, HDIM) * jax.nn.silu(gate_z).reshape(length, HEADS, HDIM)
    gated = gated * lax.rsqrt(jnp.mean(gated * gated, axis=-1, keepdims=True) + EPS_HEAD)
    gated = (
        (gated * out_gain[layer_index].reshape(HEADS, HDIM))
        .astype(jnp.bfloat16)
        .reshape(length, INNER)
    )
    return (
        seq_x.astype(jnp.float32)
        + jnp.dot(gated, w_out[layer_index], preferred_element_type=jnp.float32)
    ).astype(jnp.bfloat16)


def body(
    tokens,
    timestep,
    col_order,
    row_order,
    w_time,
    w_in,
    w_dt,
    conv_w,
    conv_b,
    dt_bias,
    a_log,
    d_skip,
    out_gain,
    w_out,
):
    params = (w_in, w_dt, conv_w, conv_b, dt_bias, a_log, d_skip, out_gain, w_out)
    condition = time_condition(timestep, w_time)
    strip_index = lax.axis_index("strip")
    strips = lax.axis_size("strip")
    frame_block = tokens[0]
    rows_here, breadth, model_width = frame_block.shape
    row_start = strip_index * rows_here
    ordered = into_order(frame_block, col_order, row_start)
    seq_first = ordered.reshape(-1, model_width)
    normed_first = modulate(seq_first, condition, 0)
    projected_first, step_first = project(normed_first, w_in, w_dt, dt_bias, 0)
    out_first = mixer(seq_first, projected_first, step_first, params, 0)
    spatial_first = from_order(
        out_first.reshape(rows_here, breadth, model_width), col_order, row_start
    )
    cols_here = breadth // strips
    split_view = spatial_first.reshape(rows_here, strips, cols_here, model_width)
    piece_rows = lax.all_to_all(split_view, "strip", split_axis=1, concat_axis=0, tiled=True)
    normed = modulate(piece_rows, condition, 1)
    projected, step_size = project(normed, w_in, w_dt, dt_bias, 1)
    col_start = strip_index * cols_here

    def to_sequence(block):
        columns_first = jnp.swapaxes(block[:, 0], 0, 1)
        arranged = into_order(columns_first, row_order, col_start)
        return arranged.reshape((-1,) + arranged.shape[2:])

    seq_second = to_sequence(piece_rows)
    out_second = mixer(seq_second, to_sequence(projected), to_sequence(step_size), params, 1)
    height = piece_rows.shape[0]
    spatial_second = from_order(
        out_second.reshape(cols_here, height, model_width), row_order, col_start
    )
    return jnp.swapaxes(spatial_second, 0, 1)[None]


def solution(mesh):
    return jax.shard_map(
        body,
        mesh=mesh,
        in_specs=(
            P("frame", "strip", None, None),
            P(),
            P(),
            P(),
            P(),
            P(),
            P(),
            P(),
            P(),
            P(),
            P(),
            P(),
            P(),
            P(),
        ),
        out_specs=P("frame", None, "strip", None),
        check_vma=False,
    )
```

profile of v0, /device:TPU:1, one launch (start us, length us, event | category | flops | bytes accessed | tf_op | source)
XLA Modules:
  0.0 909.0 jit_solution(10905470388556062400)
XLA Ops:
  8.0 1.4 copy.252
  9.4 1.4 gather_fusion.2
  13.8 4.0 fusion.3
  17.8 1.7 copy-done.3
  20.1 4.4 collective-permute-start
  28.8 1.6 copy.196
  31.2 2.1 multiply_convert_fusion.5
  35.1 3.0 divide_multiply_fusion.1
  38.1 3.1 copy.201
  42.3 49.9 %all-gather = f32[128,24,1]{1,2,0:T(1,128)S(1)} all-gather(f32[1,24,1]{1,2,0:T(1,128)S(1)} %copy.194), channel_id=2, replica_groups=mesh['frame'=8,'strip'=16] {'frame','strip'}, dimensions={0}, use_global_device_ids=true | all-gather | bytes 12384 | tf_op jit(solution)/shard_map/all_gather | solution.py:28
  95.3 1.4 fusion.110
  96.7 3.1 copy.199
  101.1 160.1 %all-gather.7.cloned.1.call-done = f32[3072,64,128]{2,1,0:T(8,128)} async-done(((f32[24,64,128]{2,1,0:T(8,128)}), f32[3072,64,128]{2,1,0:T(8,128)}) %all-gather.7.cloned.1.call-update) | async-done | bytes 100663312 | tf_op jit(solution)/shard_map/all_gather | solution.py:28
  261.2 170.8 %while.18 = (s32[]{:T(128)}, f32[24,64,128]{2,1,0:T(8,128)S(1)}, s32[]{:T(128)}, f32[128,24]{1,0:T(8,128)S(1)}, f32[128,24,64,128]{3,2,1,0:T(8,128)}, /*index=5*/s32[]{:T(128)}, s32[]{:T(128)}) while((s32[]{:T(128)}, f32[24,64,128]{2,1,0:T(8,128)S(1)}, s32[]{:T(128)}, f32[128,24]{1,0:T(8,128)S(1)}, f32[128,24,64,128]{3,2,1,0:T(8,128)}, ...), condition=%wide.region_4.6_spmd.clone, body=%wide.region_3.5_spmd.clone.sunk | while | flops 786436 | bytes 2359689 | solution.py:37
  261.2 1.3 fusion.127
  266.6 1.3 fusion.127
  267.9 1.3 fusion.127
  269.3 1.3 fusion.127
  274.6 1.3 fusion.127
  276.0 1.3 fusion.127
  277.3 1.3 fusion.127
  278.7 1.3 fusion.127
  282.7 1.3 fusion.127
  284.1 1.3 fusion.127
  285.4 1.3 fusion.127
  286.8 1.3 fusion.127
  292.1 1.3 fusion.127
  293.5 1.3 fusion.127
  294.8 1.3 fusion.127
  300.2 1.3 fusion.127
  301.6 1.3 fusion.127
  302.9 1.3 fusion.127
  304.2 1.3 fusion.127
  308.3 1.3 fusion.127
  309.6 1.3 fusion.127
  311.0 1.3 fusion.127
  312.3 1.3 fusion.127
  317.7 1.3 fusion.127
  319.0 1.3 fusion.127
  433.6 3.8 fusion.50
  437.6 1.6 copy.202
  439.2 1.6 copy.200
  440.9 3.7 fusion.60
  445.7 1.5 gather_fusion.3
  448.5 4.4 all-to-all-start
  453.1 9.2 %all-to-all-done = bf16[2,16,8,768]{3,2,0,1:T(8,128)(2,1)S(1)} async-done(((bf16[2,16,8,768]{3,2,0,1:T(8,128)(2,1)}), bf16[2,16,8,768]{3,2,0,1:T(8,128)(2,1)S(1)}, u32[]{:S(2)}, u32[]{:S(2)}) %all-to-all-start) | async-done | bytes 393248 | tf_op jit(solution)/shard_map/all_to_all | solution.py:197
  465.0 5.7 convolution_bitcast_fusion
  471.8 4.5 gather_fusion
  476.3 2.3 select_bitcast_fusion
  480.6 2.4 collective-permute-start.1
  483.9 1.6 copy.218
  485.6 3.9 collective-permute-done.1
  489.5 2.1 multiply_convert_fusion.4
  494.4 3.0 divide_multiply_fusion
  497.4 3.1 copy.223
  502.7 48.2 %all-gather.2 = f32[128,24,1]{1,2,0:T(1,128)S(1)} all-gather(f32[1,24,1]{1,2,0:T(1,128)S(1)} %copy.216), channel_id=4, replica_groups=mesh['frame'=8,'strip'=16] {'frame','strip'}, dimensions={0}, use_global_device_ids=true | all-gather | bytes 12384 | tf_op jit(solution)/shard_map/all_gather | solution.py:28
  550.9 1.4 fusion.109
  552.3 3.1 copy.221
  556.7 159.5 %all-gather.9.cloned.1.call-done = f32[3072,64,128]{2,1,0:T(8,128)} async-done(((f32[24,64,128]{2,1,0:T(8,128)}), f32[3072,64,128]{2,1,0:T(8,128)}) %all-gather.9.cloned.1.call-update) | async-done | bytes 100663312 | tf_op jit(solution)/shard_map/all_gather | solution.py:28
  716.2 170.8 %while.19 = (s32[]{:T(128)}, f32[24,64,128]{2,1,0:T(8,128)S(1)}, s32[]{:T(128)}, f32[128,24]{1,0:T(8,128)S(1)}, f32[128,24,64,128]{3,2,1,0:T(8,128)}, /*index=5*/s32[]{:T(128)}, s32[]{:T(128)}) while((s32[]{:T(128)}, f32[24,64,128]{2,1,0:T(8,128)S(1)}, s32[]{:T(128)}, f32[128,24]{1,0:T(8,128)S(1)}, ...), condition=%wide.region_11.14_spmd.clone, body=%wide.region_10.13_spmd.clone.sunk | while | flops 786436 | bytes 2359689 | solution.py:37
  888.6 3.8 fusion.48
  892.6 1.6 copy.224
  894.2 1.6 copy.222
  895.9 4.4 fusion.57
  (699 shorter events, 338.2 us)
Async XLA Ops:
  6.5 6.0 copy-start
  6.5 254.6 %all-gather.7.cloned.1.call-start = ((), (), s32[]{:S(2)}) async-start(), calls=%async_computation.1 | async-start | bytes 101449728 | tf_op jit(solution)/shard_map/all_gather | solution.py:28
  7.3 2.1 copy-start.41
  8.0 3.8 copy-start.33
  11.8 1.9 copy-start.11
  13.7 10.7 %copy-start.36 = (f32[2,24]{1,0:T(2,128)S(1)}, f32[2,24]{1,0:T(2,128)}, u32[]{:S(2)}) copy-start(f32[2,24]{1,0:T(2,128)} %param.31) | copy-start | bytes 580
  13.7 11.3 %copy-start.37 = (f32[2,24]{1,0:T(2,128)S(1)}, f32[2,24]{1,0:T(2,128)}, u32[]{:S(2)}) copy-start(f32[2,24]{1,0:T(2,128)} %param.32) | copy-start | bytes 580
  13.7 11.9 %copy-start.23 = (bf16[2,768,24]{1,2,0:T(8,128)(2,1)S(1)}, bf16[2,768,24]{1,2,0:T(8,128)(2,1)}, u32[]{:S(2)}) copy-start(bf16[2,768,24]{1,2,0:T(8,128)(2,1)} %param.28) | copy-start | bytes 221188
  13.7 14.1 %copy-start.17 = (f32[2,4,1792]{2,1,0:T(4,128)S(1)}, f32[2,4,1792]{2,1,0:T(4,128)}, u32[]{:S(2)}) copy-start(f32[2,4,1792]{2,1,0:T(4,128)} %param.29) | copy-start | bytes 172036
  13.8 14.8 %copy-start.27 = (f32[2,1792]{1,0:T(2,128)S(1)}, f32[2,1792]{1,0:T(2,128)}, u32[]{:S(2)}) copy-start(f32[2,1792]{1,0:T(2,128)} %param.30) | copy-start | bytes 43012
  17.8 1.7 copy-start.3
  20.1 11.1 %collective-permute-start = (f32[3,1792]{1,0:T(4,128)}, f32[3,1792]{1,0:T(4,128)}, u32[]{:S(2)}, u32[]{:S(2)}) collective-permute-start(f32[3,1792]{1,0:T(4,128)} %slice.227), channel_id=1, source_target_pairs={{0,1},{1,2},{2,3},{3,4},{4,5},{5,6},{6,7},{7,8},{8,9},{9,10},{10,1... | collective-permute-start | bytes 64520 | tf_op jit(solution)/shard_map/ppermute | solution.py:23
  28.8 2.4 slice-start
  30.4 2.8 copy-start.5
  38.1 54.8 %copy-start.28 = (f32[2,1536]{1,0:T(2,128)S(1)}, f32[2,1536]{1,0:T(2,128)}, u32[]{:S(2)}) copy-start(f32[2,1536]{1,0:T(2,128)} %param.34) | copy-start | bytes 36868
  38.1 56.1 %copy-start.45 = (s32[32]{0:T(128)S(1)}, s32[32]{0:T(128)}, u32[]{:S(2)}) copy-start(s32[32]{0:T(128)} %param.25) | copy-start | bytes 388
  38.1 56.6 %copy-start.38 = (f32[2,24]{1,0:T(2,128)S(1)}, f32[2,24]{1,0:T(2,128)}, u32[]{:S(2)}) copy-start(f32[2,24]{1,0:T(2,128)} %param.33) | copy-start | bytes 580
  92.9 339.9 %copy-start.15 = (pred[256,256]{1,0:T(8,128)(4,1)}, pred[256,256]{1,0:T(8,128)(4,1)S(1)}, u32[]{:S(2)}) copy-start(pred[256,256]{1,0:T(8,128)(4,1)S(1)} %iota_compare_fusion) | copy-start | bytes 196612
  432.0 1.4 copy-start.8
  432.0 1.6 copy-start.14
  432.0 1.6 copy-start.21
  439.2 1.6 copy-start.10
  439.2 1.7 copy-start.12
  440.9 4.2 copy-start.34
  444.7 2.6 copy-start.44
  445.3 7.8 copy-start.40
  445.3 7.8 copy-start.46
  445.7 16.9 %copy-start.25 = (f32[768]{0:T(1024)S(1)}, f32[768]{0:T(1024)}, u32[]{:S(2)}) copy-start(f32[768]{0:T(1024)} %get-tuple-element.366) | copy-start | bytes 9220
  445.7 16.9 %copy-start.26 = (f32[768]{0:T(1024)S(1)}, f32[768]{0:T(1024)}, u32[]{:S(2)}) copy-start(f32[768]{0:T(1024)} %get-tuple-element.367) | copy-start | bytes 9220
  447.3 15.6 %copy-start.24 = (bf16[2,768,24]{1,2,0:T(8,128)(2,1)S(1)}, bf16[2,768,24]{1,2,0:T(8,128)(2,1)}, u32[]{:S(2)}) copy-start(bf16[2,768,24]{1,2,0:T(8,128)(2,1)} %param.28) | copy-start | bytes 221188
  447.3 15.6 %copy-start.43 = (f32[24]{0:T(128)S(1)}, f32[24]{0:T(128)}, u32[]{:S(2)}) copy-start(f32[24]{0:T(128)} %get-tuple-element.374) | copy-start | bytes 292
  448.5 15.6 %copy-start.35 = (f32[24]{0:T(128)S(1)}, f32[24]{0:T(128)}, u32[]{:S(2)}) copy-start(f32[24]{0:T(128)} %get-tuple-element.372) | copy-start | bytes 292
  448.5 13.7 %all-to-all-start = ((bf16[2,16,8,768]{3,2,0,1:T(8,128)(2,1)}), bf16[2,16,8,768]{3,2,0,1:T(8,128)(2,1)S(1)}, u32[]{:S(2)}, u32[]{:S(2)}) async-start(bf16[2,16,8,768]{3,2,0,1:T(8,128)(2,1)} %copy.204), calls=%async_computation | async-start | bytes 786432 | tf_op jit(solution)/shard_map/all_to_all | solution.py:197
  453.0 263.2 %all-gather.9.cloned.1.call-start = ((), (), s32[]{:S(2)}) async-start(), calls=%async_computation.2 | async-start | bytes 101449728 | tf_op jit(solution)/shard_map/all_gather | solution.py:28
  453.1 18.7 %copy-start.30 = (s32[1024]{0:T(1024)}, s32[1024]{0:T(1024)S(1)}, u32[]{:S(2)}) copy-start(s32[1024]{0:T(1024)S(1)} %pad_clamp_fusion.1) | copy-start | bytes 12292
  453.1 23.2 %copy-start.31 = (pred[32]{0:T(512)(128)(4,1)}, pred[32]{0:T(512)(128)(4,1)S(1)}, u32[]{:S(2)}) copy-start(pred[32]{0:T(512)(128)(4,1)S(1)} %compare_and_fusion.1) | copy-start | bytes 100
  462.3 8.4 copy-start.6
  480.0 3.8 copy-start.2
  480.6 8.8 collective-permute-start.1
  483.9 5.6 copy-start.18
  483.9 5.6 copy-start.19
  483.9 5.6 copy-start.20
  485.6 6.0 copy-start.4
  491.5 0.6 copy-start.39
  497.4 3.1 copy-start.7
  497.4 3.8 copy-start.32
  716.2 171.7 %copy-start.22 = (f32[256,24]{0,1:T(8,128)S(1)}, f32[256,24]{0,1:T(8,128)}, u32[]{:S(2)}) copy-start(f32[256,24]{0,1:T(8,128)} %get-tuple-element.352) | copy-start | bytes 73732
  887.0 1.4 copy-start.9
  887.0 1.6 copy-start.13
  887.0 1.6 copy-start.16
  887.0 1.6 copy-start.42
  894.2 1.6 copy-start.29
  895.9 6.3 copy-start.1
Sparse Core Ops, SparseCore 0:
  35.1 225.9 all-gather.6
  493.6 222.5 all-gather.8
where the time goes:
time: 921 us; the launch traced here: 909 us
  other arithmetic  358 us (39%)
  waiting for transfers between devices  333 us (36%)
  blocking collectives  98.1 us (11%)
  local copies, waits for them, and re-layouts  54.8 us (6%)
  matrix products  30.7 us (3%)
  between operations  15.1 us (2%)
  starting transfers between devices  11.2 us (1%)
    select_n x254, other arithmetic, turn(): jnp.where(position < mine, new, old)  331 us
    all_gather x2, waiting for transfers between devices, prefix(): pieces = jax.tree.map(lambda part: lax.all_gather(part, axis), value)  320 us
    all_gather x2, blocking collectives, prefix(): pieces = jax.tree.map(lambda part: lax.all_gather(part, axis), value)  98.1 us
  transfers between devices with their start and end apart: 5, of which 5 were waited for; matrix products, arithmetic and copies ran while one was open for 4% of the time, Pallas kernels for 0%

commit v1 on v0

v1 whole, which is shorter than its diff:
```python
import functools
import math

import jax
import jax.numpy as jnp
from jax import lax
from jax.experimental import pallas as pl
from jax.experimental.pallas import tpu as pltpu
from jax.sharding import PartitionSpec as P

HEADS = 24
HDIM = 64
STATE = 128
CONV = 4
GROUP = 256
INNER = 1536
CONVW = 1792
WIDTH = 768
PAIRS = INNER // 128
LAYERS = 2
EPS_TOKEN = 1e-06
EPS_HEAD = 1e-05
MESH = pl.DeviceIdType.MESH
F32 = jnp.float32
BF16 = jnp.bfloat16


def time_condition(timestep, w_time):
    half_freq = w_time.shape[0] // 2
    ladder = jnp.arange(half_freq).astype(F32)
    frequency = jnp.exp(-math.log(10000.0) * ladder / half_freq)
    angles = timestep.astype(F32)[:, None] * frequency[None, :]
    feature = jnp.concatenate([jnp.cos(angles), jnp.sin(angles)], axis=1)
    feature = jax.nn.silu(feature).astype(BF16)
    return jnp.dot(feature, w_time, preferred_element_type=F32)[0]


def dot(a, b):
    return jnp.dot(a, b, preferred_element_type=F32)


def dot_rows(a, b):
    return lax.dot_general(a, b, (((0,), (0,)), ((), ())), preferred_element_type=F32)


def dot_lanes(a, b):
    return lax.dot_general(a, b, (((1,), (1,)), ((), ())), preferred_element_type=F32)


def split(value):
    high = value.astype(BF16).astype(F32)
    rest = value - high
    middle = rest.astype(BF16).astype(F32)
    return high, middle, rest - middle


def packed(value):
    lane = lax.broadcasted_iota(jnp.int32, value.shape, 1)
    high, middle, low = split(value)
    low = jnp.where(lane < 3 * HEADS, low, 0.0)
    return jnp.where(lane < HEADS, high, jnp.where(lane < 2 * HEADS, middle, low)).astype(BF16)


def softplus(value):
    return jnp.maximum(value, 0.0) + jnp.log1p(jnp.exp(-jnp.abs(value)))


def kernel(
    strips,
    frames,
    tokens_ref,
    perm_ref,
    cond_ref,
    w_dt_ref,
    small_ref,
    conv_w_ref,
    conv_b_ref,
    gain_ref,
    w_in_ref,
    w_out_ref,
    out_ref,
    xin,
    w_in,
    w_out,
    conv,
    halo,
    gate,
    xbc,
    ssd,
    weighted,
    cum_rows,
    step_rows,
    scores,
    spread,
    gather,
    lower,
    state_send,
    state_recv,
    decay_send,
    decay_recv,
    local,
    reach,
    reach_wide,
    total_send,
    total_recv,
    fdecay_send,
    fdecay_recv,
    back_send,
    back_recv,
    tok_send,
    load_sem,
    halo_sem,
    decay_sem,
    state_sem,
    fdecay_sem,
    total_sem,
    back_sem,
    tok_sem,
):
    me_f = lax.axis_index("frame")
    me_s = lax.axis_index("strip")
    rank = me_f * strips + me_s
    count = strips * frames
    after = lax.rem(rank + 1, count)
    before = lax.rem(rank + count - 1, count)
    next_id = (lax.div(after, strips), lax.rem(after, strips))
    prev_id = (lax.div(before, strips), lax.rem(before, strips))

    def load(source, target, slot):
        return pltpu.make_async_copy(source, target, load_sem.at[slot])

    loads = [
        load(tokens_ref, xin.at[0], 0),
        load(w_in_ref.at[0], w_in.at[0], 1),
        load(w_out_ref.at[0], w_out.at[0], 2),
        load(w_in_ref.at[1], w_in.at[1], 3),
        load(w_out_ref.at[1], w_out.at[1], 4),
    ]
    for item in loads:
        item.start()

    barrier = pltpu.get_barrier_semaphore()

    def greet_strip(k, carry):
        pl.semaphore_signal(
            barrier, inc=1, device_id=(me_f, lax.rem(me_s + k, strips)), device_id_type=MESH
        )
        return carry

    def greet_frame(k, carry):
        pl.semaphore_signal(
            barrier, inc=1, device_id=(lax.rem(me_f + k, frames), me_s), device_id_type=MESH
        )
        return carry

    lax.fori_loop(1, strips, greet_strip, 0)
    lax.fori_loop(1, frames, greet_frame, 0)
    pl.semaphore_signal(barrier, inc=1, device_id=next_id, device_id_type=MESH)
    pl.semaphore_signal(barrier, inc=1, device_id=prev_id, device_id_type=MESH)

    k_id = lax.broadcasted_iota(jnp.int32, (128, INNER), 0)
    c_head = lax.broadcasted_iota(jnp.int32, (128, INNER), 1) // HDIM
    hit = (c_head == k_id) | (c_head + HEADS == k_id) | (c_head + 2 * HEADS == k_id)
    spread[...] = jnp.where(hit, 1.0, 0.0).astype(BF16)
    r_head = lax.broadcasted_iota(jnp.int32, (INNER, 128), 0) // HDIM
    l_id = lax.broadcasted_iota(jnp.int32, (INNER, 128), 1)
    hit = (r_head == l_id) | (r_head + HEADS == l_id) | (r_head + 2 * HEADS == l_id)
    gather[...] = jnp.where(hit, 1.0, 0.0).astype(BF16)
    row_id = lax.broadcasted_iota(jnp.int32, (GROUP, GROUP), 0)
    col_id = lax.broadcasted_iota(jnp.int32, (GROUP, GROUP), 1)
    lower[...] = jnp.where(row_id >= col_id, 1.0, 0.0).astype(BF16)

    def peer_copy(source, target, sem, layer, k, axis):
        if axis == "strip":
            device = (me_f, lax.rem(me_s + k, strips))
        else:
            device = (lax.rem(me_f + k, frames), me_s)
        return pltpu.make_async_remote_copy(
            src_ref=source,
            dst_ref=target,
            send_sem=sem.at[layer, 0, k],
            recv_sem=sem.at[layer, 1, k],
            device_id=device,
            device_id_type=MESH,
        )

    def strip_copies(source_of, target, sem, layer):
        def make(k):
            return peer_copy(source_of(lax.rem(me_s + k, strips)), target, sem, layer, k, "strip")

        return make, strips

    def frame_copies(source, target, sem, layer):
        def make(k):
            return peer_copy(source, target, sem, layer, k, "frame")

        return make, frames

    def start(copies):
        make, n = copies

        def one(k, carry):
            make(k).start()
            return carry

        lax.fori_loop(1, n, one, 0)

    def wait(copies):
        make, n = copies

        def one(k, carry):
            make(k).wait()
            return carry

        lax.fori_loop(1, n, one, 0)

    def run_layer(layer, carry):
        @pl.when(layer == 0)
        def _():
            loads[0].wait()

        x_rows = xin[layer].reshape(GROUP, WIDTH)
        seq_x = dot(perm_ref[2 * layer], x_rows)
        mean = jnp.mean(seq_x * seq_x, axis=-1, keepdims=True)
        normed = seq_x * lax.rsqrt(mean + EPS_TOKEN)
        normed = normed * (1.0 + cond_ref[2 * layer]) + cond_ref[2 * layer + 1]
        normed = normed.astype(BF16)

        step = softplus(dot(normed, w_dt_ref[layer]) + small_ref[layer, 0:1, :])
        log_rate = -jnp.exp(small_ref[layer, 1:2, :]) * step
        high, middle, low = split(log_rate)
        triangle = lower[...]
        cum = (
            dot(triangle, high.astype(BF16))
            + dot(triangle, middle.astype(BF16))
            + dot(triangle, low.astype(BF16))
        )
        cum_end = cum[GROUP - 1 : GROUP, :]
        decay_send[layer] = jnp.broadcast_to(cum_end, (8, 128))
        decay_recv[layer, me_s] = jnp.broadcast_to(cum_end, (8, 128))

        @pl.when(layer == 0)
        def _():
            pl.semaphore_wait(barrier, strips + frames)

        decay_out = strip_copies(
            lambda peer: decay_send.at[layer], decay_recv.at[layer, me_s], decay_sem, layer
        )
        start(decay_out)

        @pl.when(layer == 0)
        def _():
            loads[1].wait()

        @pl.when(layer == 1)
        def _():
            loads[3].wait()

        def conv_tile(i, carry):
            at = pl.multiple_of(i * 256, 256)
            conv[pl.ds(8, GROUP), pl.ds(at, 256)] = dot(
                normed, w_in[layer, :, pl.ds(pl.multiple_of(INNER + at, 256), 256)]
            )
            return carry

        lax.fori_loop(0, CONVW // 256, conv_tile, 0)
        halo_out = pltpu.make_async_remote_copy(
            src_ref=conv.at[pl.ds(GROUP, 8)],
            dst_ref=halo.at[layer],
            send_sem=halo_sem.at[layer, 0],
            recv_sem=halo_sem.at[layer, 1],
            device_id=next_id,
            device_id_type=MESH,
        )
        halo_out.start()

        def gate_tile(i, carry):
            at = pl.multiple_of(i * 256, 256)
            value = dot(normed, w_in[layer, :, pl.ds(at, 256)])
            gate[:, pl.ds(at, 256)] = value * jax.nn.sigmoid(value)
            return carry

        lax.fori_loop(0, INNER // 256, gate_tile, 0)
        cum_rows[...] = cum.T
        step_rows[...] = step.T
        cum_packed = packed(cum)
        end_packed = packed(jnp.exp(cum_end - cum) * step)
        halo_out.wait()
        conv[pl.ds(0, 8), :] = jnp.where(rank == 0, 0.0, halo[layer])

        def conv_chunk(i, carry):
            at = pl.multiple_of(i * 128, 128)
            lanes = pl.ds(at, 128)
            value = conv_b_ref[layer, :, lanes]
            for tap in range(CONV):
                value = value + conv_w_ref[layer, tap : tap + 1, lanes] * conv[
                    pl.ds(9 - CONV + tap, GROUP), lanes
                ]
            xbc[:, lanes] = (value * jax.nn.sigmoid(value)).astype(BF16)
            return carry

        lax.fori_loop(0, CONVW // 128, conv_chunk, 0)

        b_rows = xbc[:, INNER : INNER + STATE]
        c_rows = xbc[:, INNER + STATE :]

        def state_tile(i, carry):
            lanes = pl.ds(pl.multiple_of(i * 256, 256), 256)
            wide = dot(end_packed, spread[:, lanes])
            piece = (xbc[:, lanes].astype(F32) * wide).astype(BF16)
            state = dot_rows(b_rows, piece)
            state_send[layer, :, :, lanes] = state.reshape(strips, 8, 256).astype(BF16)
            return carry

        lax.fori_loop(0, INNER // 256, state_tile, 0)
        state_recv[layer, me_s] = state_send[layer, me_s]
        state_out = strip_copies(
            lambda peer: state_send.at[layer, peer], state_recv.at[layer, me_s], state_sem, layer
        )
        start(state_out)

        scores[...] = dot_lanes(c_rows, b_rows)
        ones = jnp.ones((128, GROUP), BF16)
        lane24 = lax.broadcasted_iota(jnp.int32, (1, 128), 1)
        half = GROUP // 2
        skip_wide = dot(packed(small_ref[layer, 8:16, :]), spread[...])
        lane128 = lax.broadcasted_iota(jnp.int32, (1, 128), 1)
        first_half = jnp.where(lane128 < HDIM, 1.0, 0.0).astype(BF16)
        second_half = jnp.where(lane128 < HDIM, 0.0, 1.0).astype(BF16)
        reach_wide[pl.ds(0, 8), :] = skip_wide

        def mix_pair(p, carry):
            lanes = pl.ds(pl.multiple_of(p * 128, 128), 128)
            x_pair = xbc[:, lanes]
            sides = (x_pair * first_half, x_pair * second_half)
            skip = reach_wide[0:1, lanes]
            top = skip * x_pair[:half].astype(F32)
            bottom = skip * x_pair[half:].astype(F32)
            for side in range(2):
                head = 2 * p + side
                mine = (lane24 == head) | (lane24 == head + HEADS) | (lane24 == head + 2 * HEADS)
                mask = jnp.where(mine, 1.0, 0.0).astype(BF16)
                column = dot(cum_packed * mask, ones)
                row = cum_rows[pl.ds(head, 1), :]
                row_step = step_rows[pl.ds(head, 1), :]
                gap = column[:half, :half] - row[:, :half]
                near = lower_mask_top
                decay = jnp.exp(jnp.where(near, gap, -jnp.inf))
                mixing = (scores[:half, :half] * decay * row_step[:, :half]).astype(BF16)
                top = top + dot(mixing, sides[side][:half])
                gap = column[half:, :] - row
                decay = jnp.exp(jnp.where(lower_mask_bottom, gap, -jnp.inf))
                mixing = (scores[half:, :] * decay * row_step).astype(BF16)
                bottom = bottom + dot(mixing, sides[side])
            ssd[pl.ds(0, half), lanes] = top
            ssd[pl.ds(half, half), lanes] = bottom
            return carry

        t_top = lax.broadcasted_iota(jnp.int32, (half, half), 0)
        s_top = lax.broadcasted_iota(jnp.int32, (half, half), 1)
        lower_mask_top = t_top >= s_top
        t_bottom = lax.broadcasted_iota(jnp.int32, (half, GROUP), 0) + half
        s_bottom = lax.broadcasted_iota(jnp.int32, (half, GROUP), 1)
        lower_mask_bottom = t_bottom >= s_bottom
        lax.fori_loop(0, PAIRS, mix_pair, 0)

        wait(decay_out)

        def reach_step(j, running):
            reach[j] = running
            return running + decay_recv[layer, j]

        frame_decay = lax.fori_loop(0, strips, reach_step, jnp.zeros((8, 128), F32))
        fdecay_send[layer] = frame_decay
        fdecay_recv[layer, me_f] = frame_decay
        fdecay_out = frame_copies(
            fdecay_send.at[layer], fdecay_recv.at[layer, me_f], fdecay_sem, layer
        )
        start(fdecay_out)
        own_decay = packed(jnp.exp(decay_recv[layer].reshape(strips * 8, 128)))
        decay_wide = dot(own_decay, spread[...]).reshape(strips, 8, INNER)
        reach_wide[...] = decay_wide.reshape(strips * 8, INNER)
        wait(state_out)

        def scan_step(j, running):
            local[j] = running
            rows = pl.ds(pl.multiple_of(j * 8, 8), 8)
            return running * reach_wide[rows, :] + state_recv[layer, j].astype(F32)

        total = lax.fori_loop(0, strips, scan_step, jnp.zeros((8, INNER), F32))
        total_send[layer] = total.astype(BF16)
        total_recv[layer, me_f] = total.astype(BF16)
        total_out = frame_copies(total_send.at[layer], total_recv.at[layer, me_f], total_sem, layer)
        start(total_out)
        reach_wide[...] = dot(packed(jnp.exp(reach[...].reshape(strips * 8, 128))), spread[...])
        wait(fdecay_out)
        fdecay_wide = dot(
            packed(jnp.exp(fdecay_recv[layer].reshape(frames * 8, 128))), spread[...]
        )
        wait(total_out)
        entering = jnp.zeros((8, INNER), F32)
        for g in range(frames - 1):
            longer = entering * fdecay_wide[8 * g : 8 * g + 8, :] + total_recv[layer, g].astype(F32)
            entering = jnp.where(g < me_f, longer, entering)

        def back_step(j, carry):
            rows = pl.ds(pl.multiple_of(j * 8, 8), 8)
            back_send[layer, j] = (local[j] + reach_wide[rows, :] * entering).astype(BF16)
            return carry

        lax.fori_loop(0, strips, back_step, 0)
        back_recv[layer, me_s] = back_send[layer, me_s]
        back_out = strip_copies(
            lambda peer: back_send.at[layer, peer], back_recv.at[layer, me_s], back_sem, layer
        )
        start(back_out)
        grow_packed = packed(jnp.exp(cum))
        wait(back_out)

        def gate_pair(p, squares):
            lanes = pl.ds(pl.multiple_of(p * 128, 128), 128)
            state = back_recv[layer, :, :, lanes].astype(F32).reshape(STATE, 128).astype(BF16)
            carried = dot(c_rows, state) * dot(grow_packed, spread[:, lanes])
            value = (ssd[:, lanes] + carried) * gate[:, lanes]
            ssd[:, lanes] = value
            square = value * value
            top = square.astype(BF16)
            rest = (square - top.astype(F32)).astype(BF16)
            sums = gather[pl.ds(pl.multiple_of(p * 128, 128), 128), :]
            return squares + dot(top, sums) + dot(rest, sums)

        squares = lax.fori_loop(0, PAIRS, gate_pair, jnp.zeros((GROUP, 128), F32))
        scale_packed = packed(lax.rsqrt(squares * (1.0 / HDIM) + EPS_HEAD))

        def norm_pair(p, carry):
            lanes = pl.ds(pl.multiple_of(p * 128, 128), 128)
            wide = dot(scale_packed, spread[:, lanes])
            value = ssd[:, lanes] * wide * gain_ref[layer, :, lanes]
            weighted[:, lanes] = value.astype(BF16)
            return carry

        lax.fori_loop(0, PAIRS, norm_pair, 0)

        @pl.when(layer == 0)
        def _():
            loads[2].wait()

        @pl.when(layer == 1)
        def _():
            loads[4].wait()

        layer_out = (seq_x + dot(weighted[...], w_out[layer])).astype(BF16)
        placed = dot(perm_ref[2 * layer + 1], layer_out).astype(BF16)

        @pl.when(layer == 0)
        def _():
            tok_send[...] = placed.reshape(strips, 16, WIDTH)
            xin[1, me_s] = tok_send[me_s]
            tok_out = strip_copies(lambda peer: tok_send.at[peer], xin.at[1, me_s], tok_sem, 0)
            start(tok_out)
            wait(tok_out)

        @pl.when(layer == 1)
        def _():
            out_ref[...] = placed

        return carry

    lax.fori_loop(0, LAYERS, run_layer, 0)


def one_hot(targets, size):
    return targets[:, :, None] == jnp.arange(size)[None, None, :]


def permutations(col_order, row_order):
    cols = jnp.stack([col_order, jnp.flip(col_order)])
    half = jnp.arange(2)[:, None]
    source_first = (half * 128 + cols).reshape(-1)
    place_first = ((cols // 8) * 16 + half * 8 + cols % 8).reshape(-1)
    rows = jnp.stack([row_order, jnp.flip(row_order)] * 4)
    col = jnp.arange(8)[:, None]
    source_second = (rows // 2 * 16 + rows % 2 * 8 + col).reshape(-1)
    place_second = (rows * 8 + col).reshape(-1)
    spots = jnp.arange(GROUP)
    return jnp.stack(
        [
            source_first[:, None] == spots[None, :],
            spots[:, None] == place_first[None, :],
            source_second[:, None] == spots[None, :],
            spots[:, None] == place_second[None, :],
        ]
    ).astype(BF16)


def thrice(value):
    padding = jnp.zeros(value.shape[:-1] + (128 - 3 * HEADS,), value.dtype)
    return jnp.concatenate([value, value, value, padding], axis=-1)


def body(
    strips,
    frames,
    tokens,
    timestep,
    col_order,
    row_order,
    w_time,
    w_in,
    w_dt,
    conv_w,
    conv_b,
    dt_bias,
    a_log,
    d_skip,
    out_gain,
    w_out,
):
    condition = time_condition(timestep, w_time).reshape(4, 1, WIDTH)
    small = jnp.concatenate(
        [
            thrice(dt_bias)[:, None],
            thrice(a_log)[:, None],
            jnp.zeros((LAYERS, 6, 128), F32),
            jnp.broadcast_to(thrice(d_skip)[:, None], (LAYERS, 8, 128)),
        ],
        axis=1,
    )
    vmem = pl.BlockSpec(memory_space=pltpu.VMEM)
    anywhere = pl.BlockSpec(memory_space=pl.ANY)
    dma = pltpu.SemaphoreType.DMA
    call = pl.pallas_call(
        functools.partial(kernel, strips, frames),
        out_shape=jax.ShapeDtypeStruct((GROUP, WIDTH), BF16),
        in_specs=[anywhere] + [vmem] * 7 + [anywhere] * 2,
        out_specs=vmem,
        scratch_shapes=[
            pltpu.VMEM((2, strips, 16, WIDTH), BF16),
            pltpu.VMEM((2, WIDTH, INNER + CONVW), BF16),
            pltpu.VMEM((2, INNER, WIDTH), BF16),
            pltpu.VMEM((GROUP + 8, CONVW), F32),
            pltpu.VMEM((2, 8, CONVW), F32),
            pltpu.VMEM((GROUP, INNER), F32),
            pltpu.VMEM((GROUP, CONVW), BF16),
            pltpu.VMEM((GROUP, INNER), F32),
            pltpu.VMEM((GROUP, INNER), BF16),
            pltpu.VMEM((128, GROUP), F32),
            pltpu.VMEM((128, GROUP), F32),
            pltpu.VMEM((GROUP, GROUP), F32),
            pltpu.VMEM((128, INNER), BF16),
            pltpu.VMEM((INNER, 128), BF16),
            pltpu.VMEM((GROUP, GROUP), BF16),
            pltpu.VMEM((2, strips, 8, INNER), BF16),
            pltpu.VMEM((2, strips, 8, INNER), BF16),
            pltpu.VMEM((2, 8, 128), F32),
            pltpu.VMEM((2, strips, 8, 128), F32),
            pltpu.VMEM((strips, 8, INNER), F32),
            pltpu.VMEM((strips, 8, 128), F32),
            pltpu.VMEM((strips * 8, INNER), F32),
            pltpu.VMEM((2, 8, INNER), BF16),
            pltpu.VMEM((2, frames, 8, INNER), BF16),
            pltpu.VMEM((2, 8, 128), F32),
            pltpu.VMEM((2, frames, 8, 128), F32),
            pltpu.VMEM((2, strips, 8, INNER), BF16),
            pltpu.VMEM((2, strips, 8, INNER), BF16),
            pltpu.VMEM((strips, 16, WIDTH), BF16),
            dma((5,)),
            dma((2, 2)),
            dma((2, 2, strips)),
            dma((2, 2, strips)),
            dma((2, 2, frames)),
            dma((2, 2, frames)),
            dma((2, 2, strips)),
            dma((1, 2, strips)),
        ],
        compiler_params=pltpu.CompilerParams(
            collective_id=0, has_side_effects=True, vmem_limit_bytes=60 * 1024 * 1024
        ),
    )
    out = call(
        tokens.reshape(strips, 16, WIDTH),
        permutations(col_order, row_order),
        condition,
        thrice(w_dt),
        small,
        conv_w,
        conv_b[:, None],
        out_gain[:, None],
        w_in,
        w_out,
    )
    return out.reshape(1, 32, 8, WIDTH)


def solution(mesh):
    strips, frames = mesh.shape["strip"], mesh.shape["frame"]
    return jax.shard_map(
        functools.partial(body, strips, frames),
        mesh=mesh,
        in_specs=(P("frame", "strip", None, None),) + (P(),) * 13,
        out_specs=P("frame", None, "strip", None),
        check_vma=False,
    )
```

time: 921 us -> 109 us (0.12); the launches traced: 909 us -> 109 us
  other arithmetic: 358 us -> 4.6 us
  waiting for transfers between devices: 333 us -> 0 us
  blocking collectives: 98.1 us -> 0 us
  Pallas kernels: 0 us -> 94.9 us
  local copies, waits for them, and re-layouts: 54.8 us -> 6.59 us
  matrix products: 30.7 us -> 1.73 us
  between operations: 15.1 us -> 0.72 us
  starting transfers between devices: 11.2 us -> 0 us
    select_n x267 -> x0, other arithmetic: 336 us -> none  [the longest x254 331 us: turn(): jnp.where(position < mine, new, old)]
    all_gather x2 -> x0, waiting for transfers between devices: 320 us -> none  [prefix(): pieces = jax.tree.map(lambda part: lax.all_gather(part, axis), value)]
    all_gather x2 -> x0, blocking collectives: 98.1 us -> none  [prefix(): pieces = jax.tree.map(lambda part: lax.all_gather(part, axis), value)]
    pallas_call x0 -> x1, Pallas kernels: none -> 94.9 us  [body(): call(tokens.reshape(strips, 16, WIDTH), permutations(col_order, row_order...]
    dot_general x15 -> x1, matrix products: 30.7 us -> 1.73 us  [time_condition(): return jnp.dot(feature, w_time, preferred_element_type=F32)[0]]
    mul x11 -> x0, local copies, waits for them, and re-layouts: 13.8 us -> none  [the longest x2 6.21 us: mixer(): jax.nn.silu(gate_z).reshape(length, HEADS, HDIM)]
    gather x6 -> x0, local copies, waits for them, and re-layouts: 9.29 us -> none  [the longest x4 7.18 us: into_order(): gathered = jnp.take(block, order, axis=1)]
  transfers between devices with their start and end apart: 5 -> 0, of which waited for: 5 -> 0; matrix products, arithmetic and copies ran while one was open for 4% -> 0% of each run, Pallas kernels for 0% -> 0%
where the time goes in v1:
time: 109 us
  Pallas kernels  94.9 us (87%)
  local copies, waits for them, and re-layouts  6.59 us (6%)
  other arithmetic  4.6 us (4%)
  matrix products  1.73 us (2%)
    pallas_call x1, Pallas kernels, body(): call(tokens.reshape(strips, 16, WIDTH), permutations(col_order, row_order...  94.9 us

profile of v1, /device:TPU:1, one launch (start us, length us, event | category | flops | bytes accessed | tf_op | source)
XLA Modules:
  0.0 108.6 jit_solution(7677927575461935671)
XLA Ops:
  0.0 0.0 copy-start
  0.0 0.8 rev.9
  0.8 0.8 stack.41
  1.6 0.1 stack.42
  1.7 0.1 add.118
  1.8 0.1 iota_compare_fusion
  1.9 0.7 rev.8
  2.7 0.7 bitcast_add_fusion.1
  3.4 0.1 iota_compare_fusion.2
  3.5 0.9 add_convert_fusion.perm_ref
  4.4 0.0 copy-start.1
  4.4 0.0 copy-start.2
  4.4 0.1 pad.15.clone
  4.5 0.9 maximum_maximum_fusion.1
  5.4 0.1 pad.2.clone
  5.5 0.7 pad_maximum_fusion.small_ref
  6.9 1.7 %fusion = f32[1,4,768]{2,0,1:T(1,128)S(1)} fusion(bf16[256,1,1]{0,1,2:T(2,128)(2,1)S(1)} %reshape.315, bf16[32,4,8,768]{3,2,1,0:T(8,128)(2,1)} %bitcast.32), kind=kOutput, calls=%fused_computation | convolution fusion | flops 1572864 | bytes 1585664 | tf_op jit(solution)/shard_map/dot_general | solution.py:35
  8.6 0.6 dot_general.9.cond_ref
  9.2 0.0 copy-done
  9.2 0.2 copy.15
  9.5 0.1 pad.19.clone
  9.5 1.1 %maximum_maximum_fusion.w_dt_ref = bf16[2,768,128]{2,1,0:T(8,128)(2,1)} fusion(bf16[2,768,24]{2,1,0:T(8,128)(2,1)S(1)} %copy.15, bf16[128]{0:T(256)(128)(2,1)S(1)} %pad.19.clone), kind=kLoop, calls=%fused_computation.4 | loop fusion | flops 1572864 | bytes 467200 | tf_op jit(solution)/shard_map/concatenate | solution.py:498
  10.6 0.0 copy-done.1
  10.6 0.6 broadcast_in_dim.37.conv_b_ref
  11.2 0.0 copy-done.2
  11.2 0.6 broadcast_in_dim.38.gain_ref
  11.9 94.9 %shard_map.136 = bf16[256,768]{1,0:T(8,128)(2,1)} custom-call(bf16[16,16,768]{2,1,0:T(8,128)(2,1)} %bitcast.34, bf16[4,256,256]{2,1,0:T(8,128)(2,1)} %add_convert_fusion.perm_ref, f32[4,1,768]{2,1,0:T(1,128)} %dot_general.9.cond_ref, bf16[2,768,128]{2,1,0:T(8,128)(2,1)} %maximum_maximum_fusion.w_dt_ref, f32[2,16,128]{2,1,0:T(8,128)} %pad_maximum_fusion.small_ref, ...), custom_call_target="tpu_custom_call" | custom-call | tf_op jit(solution)/shard_map/pallas_call | solution.py:580
  106.8 1.8 %copy.30 = bf16[1,32,8,768]{3,2,1,0:T(8,128)(2,1)} copy(bf16[1,32,8,768]{3,2,1,0:T(8,128)(2,1)} %bitcast.33) | data formatting | bytes 786432
  (12 shorter events, 0.1 us)
Async XLA Ops:
  0.0 9.2 %copy-start = (bf16[2,768,24]{1,2,0:T(8,128)(2,1)S(1)}, bf16[2,768,24]{1,2,0:T(8,128)(2,1)}, u32[]{:S(2)}) copy-start(bf16[2,768,24]{1,2,0:T(8,128)(2,1)} %param.20) | copy-start | bytes 221188
  4.4 6.2 %copy-start.1 = (f32[2,1792]{1,0:T(2,128)S(1)}, f32[2,1792]{1,0:T(2,128)}, u32[]{:S(2)}) copy-start(f32[2,1792]{1,0:T(2,128)} %param.22) | copy-start | bytes 43012
  4.4 6.8 %copy-start.2 = (f32[2,1536]{1,0:T(2,128)S(1)}, f32[2,1536]{1,0:T(2,128)}, u32[]{:S(2)}) copy-start(f32[2,1536]{1,0:T(2,128)} %param.26) | copy-start | bytes 36868

commit v2 on v1

v2 whole, which is shorter than its diff:
```python
import functools
import math

import jax
import jax.numpy as jnp
from jax import lax
from jax.experimental import pallas as pl
from jax.experimental.pallas import tpu as pltpu
from jax.sharding import PartitionSpec as P

HEADS = 24
HDIM = 64
STATE = 128
CONV = 4
GROUP = 256
INNER = 1536
CONVW = 1792
WIDTH = 768
LAYERS = 2
SUB = 128
LOG2E = math.log2(math.e)
EPS_TOKEN = 1e-06
EPS_HEAD = 1e-05
MESH = pl.DeviceIdType.MESH
F32 = jnp.float32
BF16 = jnp.bfloat16


def dot(a, b):
    return jnp.dot(a, b, preferred_element_type=F32)


def dot_rows(a, b):
    return lax.dot_general(a, b, (((0,), (0,)), ((), ())), preferred_element_type=F32)


def dot_lanes(a, b):
    return lax.dot_general(a, b, (((1,), (1,)), ((), ())), preferred_element_type=F32)


def split(value):
    high = value.astype(BF16).astype(F32)
    rest = value - high
    middle = rest.astype(BF16).astype(F32)
    return high, middle, rest - middle


def packed(value):
    lane = lax.broadcasted_iota(jnp.int32, value.shape, 1)
    high, middle, low = split(value)
    low = jnp.where(lane < 3 * HEADS, low, 0.0)
    return jnp.where(lane < HEADS, high, jnp.where(lane < 2 * HEADS, middle, low)).astype(BF16)


def softplus(value):
    return jnp.maximum(value, 0.0) + jnp.log1p(jnp.exp(-jnp.abs(value)))


def kernel(
    strips,
    frames,
    time_ref,
    col_ref,
    row_ref,
    w_dt_ref,
    dt_bias_ref,
    a_log_ref,
    d_skip_ref,
    conv_w_ref,
    conv_b_ref,
    gain_ref,
    tokens_ref,
    w_time_ref,
    w_in_ref,
    w_out_ref,
    out_ref,
    xin,
    w_time,
    w_in,
    w_out,
    cond,
    perm,
    w_dt,
    conv,
    halo,
    gate,
    grow,
    xbc,
    ssd,
    gated,
    spread,
    block_ones,
    lower,
    half_state,
    state_send,
    state_recv,
    decay_send,
    decay_recv,
    local,
    reach,
    decay_wide,
    reach_wide,
    total_send,
    total_recv,
    fdecay_send,
    fdecay_recv,
    back_send,
    back_recv,
    tok_send,
    load_sem,
    halo_sem,
    decay_sem,
    state_sem,
    fdecay_sem,
    total_sem,
    back_sem,
    tok_sem,
):
    me_f = lax.axis_index("frame")
    me_s = lax.axis_index("strip")
    rank = me_f * strips + me_s
    count = strips * frames
    after = lax.rem(rank + 1, count)
    before = lax.rem(rank + count - 1, count)
    next_id = (lax.div(after, strips), lax.rem(after, strips))
    prev_id = (lax.div(before, strips), lax.rem(before, strips))

    def load(source, target, slot):
        return pltpu.make_async_copy(source, target, load_sem.at[slot])

    loads = [
        load(tokens_ref, xin.at[0], 0),
        load(w_in_ref.at[0], w_in.at[0], 1),
        load(w_out_ref.at[0], w_out.at[0], 2),
        load(w_in_ref.at[1], w_in.at[1], 3),
        load(w_out_ref.at[1], w_out.at[1], 4),
        load(w_time_ref, w_time, 5),
    ]
    for slot in (0, 5, 1, 2, 3, 4):
        loads[slot].start()

    barrier = pltpu.get_barrier_semaphore()

    def greet_strip(k, carry):
        pl.semaphore_signal(
            barrier, inc=1, device_id=(me_f, lax.rem(me_s + k, strips)), device_id_type=MESH
        )
        return carry

    def greet_frame(k, carry):
        pl.semaphore_signal(
            barrier, inc=1, device_id=(lax.rem(me_f + k, frames), me_s), device_id_type=MESH
        )
        return carry

    lax.fori_loop(1, strips, greet_strip, 0)
    lax.fori_loop(1, frames, greet_frame, 0)
    pl.semaphore_signal(barrier, inc=1, device_id=next_id, device_id_type=MESH)
    pl.semaphore_signal(barrier, inc=1, device_id=prev_id, device_id_type=MESH)

    def iota(shape, axis):
        return lax.broadcasted_iota(jnp.int32, shape, axis)

    def flag(hit):
        return jnp.where(hit, 1.0, 0.0).astype(BF16)

    spot = iota((128, GROUP), 1)
    pick = iota((128, GROUP), 0)
    turn = lax.shift_right_logical(spot, 7)
    step_in = spot & 127
    table = flag(pick == jnp.where(turn == 0, step_in, 127 - step_in))
    order = jnp.broadcast_to(col_ref[...].astype(F32), (8, 128)).astype(BF16)
    col = dot(order, table)[0:1].astype(jnp.int32)
    half = lax.shift_right_logical(spot[0:1], 7)
    source_first = half * 128 + col
    place_first = lax.shift_right_logical(col, 3) * 16 + half * 8 + (col & 7)
    spot = iota((32, GROUP), 1)
    pick = iota((32, GROUP), 0)
    turn = lax.shift_right_logical(spot, 5) & 1
    step_in = spot & 31
    table = flag(pick == jnp.where(turn == 0, step_in, 31 - step_in))
    order = jnp.broadcast_to(row_ref[...].astype(F32), (8, 32)).astype(BF16)
    row = dot(order, table)[0:1].astype(jnp.int32)
    column = lax.shift_right_logical(spot[0:1], 5)
    source_second = lax.shift_right_logical(row, 1) * 16 + (row & 1) * 8 + column
    place_second = row * 8 + column
    spots = iota((GROUP, GROUP), 0)
    for slot, target in enumerate((source_first, place_first, source_second, place_second)):
        perm[slot] = flag(spots == target)

    ladder = iota((8, 128), 1).astype(F32)
    angles = time_ref[0].astype(F32) * jnp.exp(-math.log(10000.0) * ladder / 128.0)
    waves = (jnp.cos(angles), jnp.sin(angles))
    feature = [(wave * jax.nn.sigmoid(wave)).astype(BF16) for wave in waves]

    k_id = iota((128, INNER), 0)
    c_head = lax.shift_right_logical(iota((128, INNER), 1), 6)
    spread[...] = flag(
        (c_head == k_id) | (c_head + HEADS == k_id) | (c_head + 2 * HEADS == k_id)
    )
    row_id = iota((GROUP, GROUP), 0)
    col_id = iota((GROUP, GROUP), 1)
    block_ones[...] = flag(
        lax.shift_right_logical(row_id, 6) == lax.shift_right_logical(col_id, 6)
    )
    lower[...] = flag(
        (row_id >= col_id)
        & (lax.shift_right_logical(row_id, 7) == lax.shift_right_logical(col_id, 7))
    )
    r_id = iota((HEADS, 128), 0)
    l_id = iota((HEADS, 128), 1)
    thrice = flag((l_id == r_id) | (l_id == r_id + HEADS) | (l_id == r_id + 2 * HEADS))
    for slot in range(LAYERS):
        w_dt[slot] = dot(w_dt_ref[slot], thrice).astype(BF16)

    def repeated(value):
        high, middle, low = split(value)
        return (
            dot(high.astype(BF16), thrice)
            + dot(middle.astype(BF16), thrice)
            + dot(low.astype(BF16), thrice)
        )

    dt_bias = repeated(dt_bias_ref[...])
    rates = -LOG2E * jnp.exp(repeated(a_log_ref[...]))
    d_skip = repeated(d_skip_ref[...])
    loads[5].wait()
    for slot in range(2 * LAYERS):
        lanes = pl.ds(slot * WIDTH, WIDTH)
        cond[slot] = dot(feature[0], w_time[:128, lanes]) + dot(feature[1], w_time[128:, lanes])

    def peer_copy(source, target, sem, layer, k, axis):
        if axis == "strip":
            device = (me_f, lax.rem(me_s + k, strips))
        else:
            device = (lax.rem(me_f + k, frames), me_s)
        return pltpu.make_async_remote_copy(
            src_ref=source,
            dst_ref=target,
            send_sem=sem.at[layer, 0, k],
            recv_sem=sem.at[layer, 1, k],
            device_id=device,
            device_id_type=MESH,
        )

    def strip_copies(source_of, target, sem, layer):
        def make(k):
            return peer_copy(source_of(lax.rem(me_s + k, strips)), target, sem, layer, k, "strip")

        return make, strips

    def frame_copies(source, target, sem, layer):
        def make(k):
            return peer_copy(source, target, sem, layer, k, "frame")

        return make, frames

    def start(copies):
        make, n = copies

        def one(k, carry):
            make(k).start()
            return carry

        lax.fori_loop(1, n, one, 0)

    def wait(copies):
        make, n = copies

        def one(k, carry):
            make(k).wait()
            return carry

        lax.fori_loop(1, n, one, 0)

    def wait_load(layer, slots):
        for number, slot in enumerate(slots):

            @pl.when(layer == number)
            def _(slot=slot):
                loads[slot].wait()

    def run_layer(layer, carry):
        def own(pair):
            return jnp.where(layer == 0, pair[0:1], pair[1:2])

        @pl.when(layer == 0)
        def _():
            loads[0].wait()

        seq_x = dot_rows(perm[2 * layer], xin[layer].reshape(GROUP, WIDTH))
        mean = jnp.mean(seq_x * seq_x, axis=-1, keepdims=True)
        normed = seq_x * lax.rsqrt(mean + EPS_TOKEN)
        normed = normed * (1.0 + cond[2 * layer, 0:1, :]) + cond[2 * layer + 1, 0:1, :]
        normed = normed.astype(BF16)

        wait_load(layer, (1, 3))
        for at in range(0, CONVW, 256):
            conv[pl.ds(8, GROUP), pl.ds(at, 256)] = dot(
                normed, w_in[layer, :, pl.ds(INNER + at, 256)]
            )

        @pl.when(layer == 0)
        def _():
            pl.semaphore_wait(barrier, strips + frames)

        halo_out = pltpu.make_async_remote_copy(
            src_ref=conv.at[pl.ds(GROUP, 8)],
            dst_ref=halo.at[layer],
            send_sem=halo_sem.at[layer, 0],
            recv_sem=halo_sem.at[layer, 1],
            device_id=next_id,
            device_id_type=MESH,
        )
        halo_out.start()

        step = softplus(dot(normed, w_dt[layer]) + own(dt_bias))
        high, middle, low = split(own(rates) * step)
        triangle = lower[...]
        cum = (
            dot(triangle, high.astype(BF16))
            + dot(triangle, middle.astype(BF16))
            + dot(triangle, low.astype(BF16))
        )
        ends = (cum[SUB - 1 : SUB, :], cum[GROUP - 1 : GROUP, :])
        cum_end = jnp.broadcast_to(ends[0] + ends[1], (8, 128))
        decay_send[layer] = cum_end
        decay_recv[layer, me_s] = cum_end
        decay_out = strip_copies(
            lambda peer: decay_send.at[layer], decay_recv.at[layer, me_s], decay_sem, layer
        )
        start(decay_out)
        sub_id = iota((GROUP, 128), 0)
        to_end = jnp.where(sub_id < SUB, ends[0], ends[1]) - cum
        end_packed = packed(jnp.exp2(to_end) * step)
        grow_packed = packed(jnp.exp2(cum))
        rows = (cum - LOG2E * jnp.log(step)).T
        heads_in = jnp.concatenate(
            [
                jnp.broadcast_to(own(d_skip), (8, 128)),
                jnp.broadcast_to(jnp.exp2(ends[0]), (8, 128)),
                jnp.broadcast_to(jnp.exp2(ends[1]), (8, 128)),
            ],
            axis=0,
        )
        heads_wide = dot(packed(heads_in), spread[...])
        skip_wide = heads_wide[0:1]
        shrink_first = heads_wide[8:9]
        shrink_second = heads_wide[16:17]
        halo_out.wait()
        conv[pl.ds(0, 8), :] = jnp.where(rank == 0, 0.0, halo[layer])

        for at in range(0, CONVW, 128):
            lanes = pl.ds(at, 128)
            value = own(conv_b_ref[:, lanes])
            for tap in range(CONV):
                value = value + conv_w_ref[layer, tap : tap + 1, lanes] * conv[
                    pl.ds(9 - CONV + tap, GROUP), lanes
                ]
            xbc[:, lanes] = (value * jax.nn.sigmoid(value)).astype(BF16)

        b_rows = xbc[:, INNER : INNER + STATE]
        c_rows = xbc[:, INNER + STATE :]
        for at in range(0, INNER, 256):
            lanes = pl.ds(at, 256)
            wide = dot(end_packed, spread[:, lanes])
            piece = (xbc[:, lanes].astype(F32) * wide).astype(BF16)
            first = dot_rows(b_rows[:SUB], piece[:SUB])
            half_state[:, lanes] = first
            state = first * shrink_second[:, at : at + 256] + dot_rows(b_rows[SUB:], piece[SUB:])
            state_send[layer, :, :, lanes] = state.reshape(strips, 8, 256).astype(BF16)
        state_recv[layer, me_s] = state_send[layer, me_s]
        state_out = strip_copies(
            lambda peer: state_send.at[layer, peer], state_recv.at[layer, me_s], state_sem, layer
        )
        start(state_out)

        near = iota((SUB, SUB), 0) >= iota((SUB, SUB), 1)
        scores = [dot_lanes(c_rows[at : at + SUB], b_rows[at : at + SUB]) for at in (0, SUB)]
        lane = iota((1, 128), 1)
        sides = (flag(lane < HDIM), flag(lane >= HDIM))

        def mix(pairs):
            for pair in pairs:
                lanes = pl.ds(pair * 128, 128)
                for block in range(2):
                    at = block * SUB
                    x_pair = xbc[pl.ds(at, SUB), lanes]
                    mixing = []
                    for side in range(2):
                        head = 2 * pair + side
                        gap = cum[at : at + SUB, head : head + 1] - rows[
                            head : head + 1, at : at + SUB
                        ]
                        decay = jnp.exp2(jnp.where(near, gap, -jnp.inf))
                        mixing.append((scores[block] * decay).astype(BF16))
                    inside = dot(
                        jnp.concatenate(mixing, axis=1),
                        jnp.concatenate([x_pair * sides[0], x_pair * sides[1]], axis=0),
                    )
                    skip = skip_wide[:, pair * 128 : pair * 128 + 128] * x_pair.astype(F32)
                    ssd[pl.ds(at, SUB), lanes] = inside + skip

        for at in range(0, INNER, 256):
            value = dot(normed, w_in[layer, :, pl.ds(at, 256)])
            gate[:, pl.ds(at, 256)] = value * jax.nn.sigmoid(value)
        mix(range(0, 4))

        wait(decay_out)
        running = jnp.zeros((8, 128), F32)
        for j in range(strips):
            reach[j] = running
            running = running + decay_recv[layer, j]
        fdecay_send[layer] = running
        fdecay_recv[layer, me_f] = running
        fdecay_out = frame_copies(
            fdecay_send.at[layer], fdecay_recv.at[layer, me_f], fdecay_sem, layer
        )
        start(fdecay_out)
        own_decay = packed(jnp.exp2(decay_recv[layer].reshape(strips * 8, 128)))
        decay_wide[...] = dot(own_decay, spread[...]).reshape(strips, 8, INNER)
        wait(state_out)
        running = jnp.zeros((8, INNER), F32)
        for j in range(strips):
            local[j] = running
            running = running * decay_wide[j] + state_recv[layer, j].astype(F32)
        total_send[layer] = running.astype(BF16)
        total_recv[layer, me_f] = running.astype(BF16)
        total_out = frame_copies(total_send.at[layer], total_recv.at[layer, me_f], total_sem, layer)
        start(total_out)
        own_reach = packed(jnp.exp2(reach[...].reshape(strips * 8, 128)))
        reach_wide[...] = dot(own_reach, spread[...]).reshape(strips, 8, INNER)
        mix(range(4, 8))
        wait(fdecay_out)
        fdecay_wide = dot(
            packed(jnp.exp2(fdecay_recv[layer].reshape(frames * 8, 128))), spread[...]
        )
        wait(total_out)
        entering = jnp.zeros((8, INNER), F32)
        for g in range(frames - 1):
            longer = entering * fdecay_wide[8 * g : 8 * g + 8, :] + total_recv[layer, g].astype(F32)
            entering = jnp.where(g < me_f, longer, entering)
        for j in range(strips):
            back_send[layer, j] = (local[j] + reach_wide[j] * entering).astype(BF16)
        back_recv[layer, me_s] = back_send[layer, me_s]
        back_out = strip_copies(
            lambda peer: back_send.at[layer, peer], back_recv.at[layer, me_s], back_sem, layer
        )
        start(back_out)
        mix(range(8, 12))
        for at in range(0, INNER, 256):
            lanes = pl.ds(at, 256)
            wide = dot(grow_packed, spread[:, lanes])
            ssd[:, lanes] = ssd[:, lanes] * gate[:, lanes]
            grow[:, lanes] = wide * gate[:, lanes]
        wait(back_out)

        for at in range(0, INNER, 256):
            lanes = pl.ds(at, 256)
            state = back_recv[layer, :, :, lanes].astype(F32).reshape(STATE, 256)
            later = state * shrink_first[:, at : at + 256] + half_state[:, lanes]
            carried = jnp.concatenate(
                [dot(c_rows[:SUB], state.astype(BF16)), dot(c_rows[SUB:], later.astype(BF16))],
                axis=0,
            )
            value = ssd[:, lanes] + carried * grow[:, lanes]
            square = value * value
            top = square.astype(BF16)
            rest = (square - top.astype(F32)).astype(BF16)
            sums = dot(top, block_ones[...]) + dot(rest, block_ones[...])
            scale = lax.rsqrt(sums * (1.0 / HDIM) + EPS_HEAD)
            gated[:, lanes] = (value * scale * own(gain_ref[:, lanes])).astype(BF16)

        wait_load(layer, (2, 4))
        layer_out = (seq_x + dot(gated[...], w_out[layer])).astype(BF16)
        placed = dot(perm[2 * layer + 1], layer_out).astype(BF16)

        @pl.when(layer == 0)
        def _():
            tok_send[...] = placed.reshape(strips, 16, WIDTH)
            xin[1, me_s] = tok_send[me_s]
            tok_out = strip_copies(lambda peer: tok_send.at[peer], xin.at[1, me_s], tok_sem, 0)
            start(tok_out)
            wait(tok_out)

        @pl.when(layer == 1)
        def _():
            out_ref[...] = placed

        return carry

    lax.fori_loop(0, LAYERS, run_layer, 0)


def body(
    strips,
    frames,
    tokens,
    timestep,
    col_order,
    row_order,
    w_time,
    w_in,
    w_dt,
    conv_w,
    conv_b,
    dt_bias,
    a_log,
    d_skip,
    out_gain,
    w_out,
):
    vmem = pl.BlockSpec(memory_space=pltpu.VMEM)
    smem = pl.BlockSpec(memory_space=pltpu.SMEM)
    anywhere = pl.BlockSpec(memory_space=pl.ANY)
    dma = pltpu.SemaphoreType.DMA
    call = pl.pallas_call(
        functools.partial(kernel, strips, frames),
        out_shape=jax.ShapeDtypeStruct((GROUP, WIDTH), BF16),
        in_specs=[smem] + [vmem] * 9 + [anywhere] * 4,
        out_specs=vmem,
        scratch_shapes=[
            pltpu.VMEM((2, strips, 16, WIDTH), BF16),
            pltpu.VMEM((256, 2 * LAYERS * WIDTH), BF16),
            pltpu.VMEM((2, WIDTH, INNER + CONVW), BF16),
            pltpu.VMEM((2, INNER, WIDTH), BF16),
            pltpu.VMEM((2 * LAYERS, 8, WIDTH), F32),
            pltpu.VMEM((2 * LAYERS, GROUP, GROUP), BF16),
            pltpu.VMEM((2, WIDTH, 128), BF16),
            pltpu.VMEM((GROUP + 8, CONVW), F32),
            pltpu.VMEM((2, 8, CONVW), F32),
            pltpu.VMEM((GROUP, INNER), F32),
            pltpu.VMEM((GROUP, INNER), F32),
            pltpu.VMEM((GROUP, CONVW), BF16),
            pltpu.VMEM((GROUP, INNER), F32),
            pltpu.VMEM((GROUP, INNER), BF16),
            pltpu.VMEM((128, INNER), BF16),
            pltpu.VMEM((GROUP, GROUP), BF16),
            pltpu.VMEM((GROUP, GROUP), BF16),
            pltpu.VMEM((STATE, INNER), F32),
            pltpu.VMEM((2, strips, 8, INNER), BF16),
            pltpu.VMEM((2, strips, 8, INNER), BF16),
            pltpu.VMEM((2, 8, 128), F32),
            pltpu.VMEM((2, strips, 8, 128), F32),
            pltpu.VMEM((strips, 8, INNER), F32),
            pltpu.VMEM((strips, 8, 128), F32),
            pltpu.VMEM((strips, 8, INNER), F32),
            pltpu.VMEM((strips, 8, INNER), F32),
            pltpu.VMEM((2, 8, INNER), BF16),
            pltpu.VMEM((2, frames, 8, INNER), BF16),
            pltpu.VMEM((2, 8, 128), F32),
            pltpu.VMEM((2, frames, 8, 128), F32),
            pltpu.VMEM((2, strips, 8, INNER), BF16),
            pltpu.VMEM((2, strips, 8, INNER), BF16),
            pltpu.VMEM((strips, 16, WIDTH), BF16),
            dma((6,)),
            dma((2, 2)),
            dma((2, 2, strips)),
            dma((2, 2, strips)),
            dma((2, 2, frames)),
            dma((2, 2, frames)),
            dma((2, 2, strips)),
            dma((1, 2, strips)),
        ],
        compiler_params=pltpu.CompilerParams(
            collective_id=0, has_side_effects=True, vmem_limit_bytes=60 * 1024 * 1024
        ),
    )
    out = call(
        timestep,
        col_order.reshape(1, 128),
        row_order.reshape(1, 32),
        w_dt,
        dt_bias,
        a_log,
        d_skip,
        conv_w,
        conv_b,
        out_gain,
        tokens.reshape(strips, 16, WIDTH),
        w_time,
        w_in,
        w_out,
    )
    return out.reshape(1, 32, 8, WIDTH)


def solution(mesh):
    strips, frames = mesh.shape["strip"], mesh.shape["frame"]
    return jax.shard_map(
        functools.partial(body, strips, frames),
        mesh=mesh,
        in_specs=(P("frame", "strip", None, None),) + (P(),) * 13,
        out_specs=P("frame", None, "strip", None),
        check_vma=False,
    )
```

time: 109 us -> 84.5 us (0.78)
  Pallas kernels: 94.9 us -> 79.6 us
  other arithmetic: 4.6 us -> 0 us
  local copies, waits for them, and re-layouts: 6.59 us -> 3.57 us
  matrix products: 1.73 us -> 0 us
    pallas_call x1, Pallas kernels: 94.9 us -> 79.6 us  [body(): call(timestep, col_order.reshape(1, 128), row_order.reshape(1, 32), w_dt,...]
    concatenate x3 -> x0, other arithmetic: 2.67 us -> none  [the longest x2 2 us: thrice(): return jnp.concatenate([value, value, value, padding], axis=-1)]
    dot_general x1 -> x0, matrix products: 1.73 us -> none  [time_condition(): return jnp.dot(feature, w_time, preferred_element_type=F32)[0]]
    unnamed x8 -> x2, local copies, waits for them, and re-layouts: 2 us -> 3.57 us
    rev x2 -> x0, local copies, waits for them, and re-layouts: 1.52 us -> none  [the longest x1 0.78 us: permutations(): rows = jnp.stack([row_order, jnp.flip(row_order)] * 4)]
    broadcast_in_dim x5 -> x0, local copies, waits for them, and re-layouts: 1.23 us -> none  [the longest x1 0.62 us: body(): out_gain[:, None]]
where the time goes in v2:
time: 84.5 us; the launch traced here: 83.8 us
  Pallas kernels  79.6 us (94%)
  local copies, waits for them, and re-layouts  3.57 us (4%)
    pallas_call x1, Pallas kernels, body(): call(timestep, col_order.reshape(1, 128), row_order.reshape(1, 32), w_dt,...  79.6 us
    unnamed x2, local copies, waits for them, and re-layouts  3.57 us

profile of v2, /device:TPU:1, one launch (start us, length us, event | category | flops | bytes accessed | tf_op | source)
XLA Modules:
  0.0 83.8 jit_solution(17138570351924219423)
XLA Ops:
  0.7 1.8 %copy.15.w_dt_ref = bf16[2,768,24]{2,1,0:T(8,128)(2,1)} copy(bf16[2,768,24]{1,2,0:T(8,128)(2,1)} %param.20) | data formatting | bytes 147456 | tf_op args[6]
  2.5 79.6 %shard_map.136 = bf16[256,768]{1,0:T(8,128)(2,1)} custom-call(s32[1]{0:T(128)S(6)} %copy.17.time_ref, s32[1,128]{1,0:T(1,128)} %bitcast.6, s32[1,32]{1,0:T(1,128)} %bitcast.7, bf16[2,768,24]{2,1,0:T(8,128)(2,1)} %copy.15.w_dt_ref, f32[2,24]{1,0:T(2,128)} %dt_bias_ref.1, f32[2,24]{1,0:T(2,128)} %a_log_ref.1, f32[2,24]{1,0:T(2,128)} %d_skip_ref.1, ...), custom_call_target="tpu_custom_call" | custom-call | tf_op jit(solution)/shard_map/pallas_call | solution.py:569
  82.1 1.8 %copy.18 = bf16[1,32,8,768]{3,2,1,0:T(8,128)(2,1)} copy(bf16[1,32,8,768]{3,2,1,0:T(8,128)(2,1)} %bitcast.4) | data formatting | bytes 786432

commit v3 on v2

--- a/solution.py
+++ b/solution.py
@@ -211,7 +211,7 @@
     l_id = iota((HEADS, 128), 1)
     thrice = flag((l_id == r_id) | (l_id == r_id + HEADS) | (l_id == r_id + 2 * HEADS))
     for slot in range(LAYERS):
-        w_dt[slot] = dot(w_dt_ref[slot], thrice).astype(BF16)
+        w_dt[slot] = dot_rows(w_dt_ref[slot], thrice).astype(BF16)
 
     def repeated(value):
         high, middle, low = split(value)
@@ -229,11 +229,28 @@
         lanes = pl.ds(slot * WIDTH, WIDTH)
         cond[slot] = dot(feature[0], w_time[:128, lanes]) + dot(feature[1], w_time[128:, lanes])
 
-    def peer_copy(source, target, sem, layer, k, axis):
-        if axis == "strip":
-            device = (me_f, lax.rem(me_s + k, strips))
-        else:
-            device = (lax.rem(me_f + k, frames), me_s)
+    side = 4
+    hops = (0, 1, 2, 1)
+    spots_x = [lax.rem(lax.div(me_s, side) + step, side) for step in range(side)]
+    spots_z = [lax.rem(lax.rem(me_s, side) + step, side) for step in range(side)]
+    strip_peers = [
+        spots_x[dx] * side + spots_z[dz]
+        for dx, dz in sorted(
+            [(dx, dz) for dx in range(side) for dz in range(side) if dx or dz],
+            key=lambda offset: -hops[offset[0]] - hops[offset[1]],
+        )
+    ]
+    spots_y = [lax.rem(lax.div(me_f, 2) + step, side) for step in range(side)]
+    spots_c = [lax.rem(lax.rem(me_f, 2) + step, 2) for step in range(2)]
+    frame_peers = [
+        spots_y[dy] * 2 + spots_c[dc]
+        for dy, dc in sorted(
+            [(dy, dc) for dy in range(side) for dc in range(2) if dy or dc],
+            key=lambda offset: -hops[offset[0]],
+        )
+    ]
+
+    def peer_copy(source, target, sem, layer, k, device):
         return pltpu.make_async_remote_copy(
             src_ref=source,
             dst_ref=target,
@@ -244,34 +261,24 @@
         )
 
     def strip_copies(source_of, target, sem, layer):
-        def make(k):
-            return peer_copy(source_of(lax.rem(me_s + k, strips)), target, sem, layer, k, "strip")
-
-        return make, strips
+        return [
+            peer_copy(source_of(peer), target, sem, layer, k, (me_f, peer))
+            for k, peer in enumerate(strip_peers)
+        ]
 
     def frame_copies(source, target, sem, layer):
-        def make(k):
-            return peer_copy(source, target, sem, layer, k, "frame")
-
-        return make, frames
+        return [
+            peer_copy(source, target, sem, layer, k, (peer, me_s))
+            for k, peer in enumerate(frame_peers)
+        ]
 
     def start(copies):
-        make, n = copies
-
-        def one(k, carry):
-            make(k).start()
-            return carry
-
-        lax.fori_loop(1, n, one, 0)
+        for item in copies:
+            item.start()
 
     def wait(copies):
-        make, n = copies
-
-        def one(k, carry):
-            make(k).wait()
-            return carry
-
-        lax.fori_loop(1, n, one, 0)
+        for item in copies:
+            item.wait()
 
     def wait_load(layer, slots):
         for number, slot in enumerate(slots):
@@ -347,27 +354,41 @@
         skip_wide = heads_wide[0:1]
         shrink_first = heads_wide[8:9]
         shrink_second = heads_wide[16:17]
+        for at in range(0, INNER, 256):
+            value = dot(normed, w_in[layer, :, pl.ds(at, 256)])
+            gate[:, pl.ds(at, 256)] = value * jax.nn.sigmoid(value)
+
+        def convolve(top, count):
+            for at in range(0, CONVW, 128):
+                lanes = pl.ds(at, 128)
+                value = own(conv_b_ref[:, lanes])
+                for tap in range(CONV):
+                    value = value + conv_w_ref[layer, tap : tap + 1, lanes] * conv[
+                        pl.ds(top + 9 - CONV + tap, count), lanes
+                    ]
+                xbc[pl.ds(top, count), lanes] = (value * jax.nn.sigmoid(value)).astype(BF16)
+
+        def sub_state(top, lanes):
+            b_part = xbc[pl.ds(top, SUB), INNER : INNER + STATE]
+            wide = dot(end_packed[top : top + SUB], spread[:, lanes])
+            piece = (xbc[pl.ds(top, SUB), lanes].astype(F32) * wide).astype(BF16)
+            return dot_rows(b_part, piece)
+
+        convolve(16, GROUP - 16)
+        for at in range(0, INNER, 256):
+            lanes = pl.ds(at, 256)
+            grow[pl.ds(0, STATE), lanes] = sub_state(SUB, lanes)
         halo_out.wait()
         conv[pl.ds(0, 8), :] = jnp.where(rank == 0, 0.0, halo[layer])
-
-        for at in range(0, CONVW, 128):
-            lanes = pl.ds(at, 128)
-            value = own(conv_b_ref[:, lanes])
-            for tap in range(CONV):
-                value = value + conv_w_ref[layer, tap : tap + 1, lanes] * conv[
-                    pl.ds(9 - CONV + tap, GROUP), lanes
-                ]
-            xbc[:, lanes] = (value * jax.nn.sigmoid(value)).astype(BF16)
+        convolve(0, 16)
 
         b_rows = xbc[:, INNER : INNER + STATE]
         c_rows = xbc[:, INNER + STATE :]
         for at in range(0, INNER, 256):
             lanes = pl.ds(at, 256)
-            wide = dot(end_packed, spread[:, lanes])
-            piece = (xbc[:, lanes].astype(F32) * wide).astype(BF16)
-            first = dot_rows(b_rows[:SUB], piece[:SUB])
+            first = sub_state(0, lanes)
             half_state[:, lanes] = first
-            state = first * shrink_second[:, at : at + 256] + dot_rows(b_rows[SUB:], piece[SUB:])
+            state = first * shrink_second[:, at : at + 256] + grow[pl.ds(0, STATE), lanes]
             state_send[layer, :, :, lanes] = state.reshape(strips, 8, 256).astype(BF16)
         state_recv[layer, me_s] = state_send[layer, me_s]
         state_out = strip_copies(
@@ -401,9 +422,6 @@
                     skip = skip_wide[:, pair * 128 : pair * 128 + 128] * x_pair.astype(F32)
                     ssd[pl.ds(at, SUB), lanes] = inside + skip
 
-        for at in range(0, INNER, 256):
-            value = dot(normed, w_in[layer, :, pl.ds(at, 256)])
-            gate[:, pl.ds(at, 256)] = value * jax.nn.sigmoid(value)
         mix(range(0, 4))
 
         wait(decay_out)
@@ -473,11 +491,11 @@
 
         wait_load(layer, (2, 4))
         layer_out = (seq_x + dot(gated[...], w_out[layer])).astype(BF16)
-        placed = dot(perm[2 * layer + 1], layer_out).astype(BF16)
+        placed = dot(perm[2 * layer + 1], layer_out)
 
         @pl.when(layer == 0)
         def _():
-            tok_send[...] = placed.reshape(strips, 16, WIDTH)
+            tok_send[...] = placed.astype(BF16).reshape(strips, 16, WIDTH)
             xin[1, me_s] = tok_send[me_s]
             tok_out = strip_copies(lambda peer: tok_send.at[peer], xin.at[1, me_s], tok_sem, 0)
             start(tok_out)
@@ -485,7 +503,7 @@
 
         @pl.when(layer == 1)
         def _():
-            out_ref[...] = placed
+            out_ref[...] = placed.reshape(32, 8, WIDTH).astype(BF16)
 
         return carry
 
@@ -516,7 +534,7 @@
     dma = pltpu.SemaphoreType.DMA
     call = pl.pallas_call(
         functools.partial(kernel, strips, frames),
-        out_shape=jax.ShapeDtypeStruct((GROUP, WIDTH), BF16),
+        out_shape=jax.ShapeDtypeStruct((32, 8, WIDTH), BF16),
         in_specs=[smem] + [vmem] * 9 + [anywhere] * 4,
         out_specs=vmem,
         scratch_shapes=[
@@ -570,7 +588,7 @@
         timestep,
         col_order.reshape(1, 128),
         row_order.reshape(1, 32),
-        w_dt,
+        jnp.swapaxes(w_dt, 1, 2),
         dt_bias,
         a_log,
         d_skip,

time: 84.5 us -> 74.9 us (0.89)
  Pallas kernels: 79.6 us -> 72.2 us
  local copies, waits for them, and re-layouts: 3.57 us -> 1.77 us
    pallas_call x1, Pallas kernels: 79.6 us -> 72.2 us  [body(): call(timestep, col_order.reshape(1, 128), row_order.reshape(1, 32), jnp.s...]
    unnamed x2 -> x1, local copies, waits for them, and re-layouts: 3.57 us -> 1.77 us
where the time goes in v3:
time: 74.9 us; the launch traced here: 74.7 us
  Pallas kernels  72.2 us (96%)
  local copies, waits for them, and re-layouts  1.77 us (2%)
    pallas_call x1, Pallas kernels, body(): call(timestep, col_order.reshape(1, 128), row_order.reshape(1, 32), jnp.s...  72.2 us
    unnamed x1, local copies, waits for them, and re-layouts  1.77 us

profile of v3, /device:TPU:1, one launch (start us, length us, event | category | flops | bytes accessed | tf_op | source)
XLA Modules:
  0.0 74.7 jit_solution(16612941955250284573)
XLA Ops:
  0.7 72.2 %shard_map.136 = bf16[32,8,768]{2,1,0:T(8,128)(2,1)} custom-call(s32[1]{0:T(128)S(6)} %copy.16.time_ref, s32[1,128]{1,0:T(1,128)} %bitcast.8, s32[1,32]{1,0:T(1,128)} %bitcast.9, bf16[2,24,768]{2,1,0:T(8,128)(2,1)} %bitcast.7, f32[2,24]{1,0:T(2,128)} %dt_bias_ref.1, f32[2,24]{1,0:T(2,128)} %a_log_ref.1, f32[2,24]{1,0:T(2,128)} %d_skip_ref.1, ...), custom_call_target="tpu_custom_call" | custom-call | tf_op jit(solution)/shard_map/pallas_call | solution.py:587
  72.9 1.8 %copy.17 = bf16[1,32,8,768]{3,2,1,0:T(8,128)(2,1)} copy(bf16[1,32,8,768]{3,2,1,0:T(8,128)(2,1)} %bitcast.5) | data formatting | bytes 786432
